TPU v7x, 512 devices: a whole 4x4x16 slice. The times are simulated.
512 devices in a mesh: dp: 32 (over z, core), member: 16 (over y, x).
Axes of the slice: x: 4, y: 4, z: 16, core: 2. Of those that a mesh axis runs over, the one named last changes fastest.
Arguments:
- tokens: bfloat16 [4096, 4096], P('dp', 'member'), may hold values from -6 to 6
- routes: int32 [4096, 2], P('dp'), may hold values from 0 to 7, all different within a row; in each aligned block of 128 rows (0 to 127, 128 to 255, ...) at most 34 rows name the same one
- route_weights: float32 [4096, 2], P('dp'), may hold values from 0.2 to 1
- up_stacked: bfloat16 [8, 4096, 7168], P(None, ('member', 'dp')), may hold values from -0.09375 to 0.09375
- down_stacked: bfloat16 [8, 4096, 7168], P(None, ('member', 'dp')), may hold values from -0.0625 to 0.0625
- cotangent: bfloat16 [4096, 4096], P('dp', 'member'), may hold values from -6 to 6
Outputs:
- mixed: bfloat16 [4096, 4096], P('dp', 'member')
- grad_tokens: bfloat16 [4096, 4096], P('dp', 'member')
- grad_up: bfloat16 [32, 4096, 1792], P('dp', 'member')
- grad_down: bfloat16 [32, 4096, 1792], P('dp', 'member')
Inputs may be any that keep to these rules, and one draw needn't show every extreme that they name: `routes`: each row names two different experts. In each aligned block of 128 rows no expert is named by more than 34 rows, and in some block some expert is named by exactly 34 rows.
All inputs are finite; a program needn't handle non-finite values.
Results may differ from a plain program's by a relative error of at most 0.018.
Values may be sent and summed in bfloat16 or wider, within the bound.
A program may use at most 64 MiB of HBM per device.

v0:
```python
import jax
import jax.numpy as jnp
from jax import lax
from jax.sharding import PartitionSpec as P

FF_W = 7168
E = 8
CAP = 34


def contract(left, right, left_dim, right_dim):
    return lax.dot_general(
        left, right, (((left_dim,), (right_dim,)), ((), ())), preferred_element_type=jnp.float32
    )


def body(tokens, routes, route_weights, up_stacked, down_stacked, cotangent):
    dp_count = lax.axis_size("dp")
    member_count = lax.axis_size("member")
    quarters = dp_count // E
    share_rows = up_stacked.shape[1]
    features = tokens.shape[1]
    hidden_own = FF_W // quarters
    per_member = hidden_own // member_count
    slots_all = E * CAP
    up_parts = (
        up_stacked.reshape(E, share_rows, quarters, hidden_own)
        .transpose(0, 2, 1, 3)
        .reshape(dp_count, share_rows, hidden_own)
    )
    down_parts = (
        down_stacked.reshape(E, share_rows, quarters, hidden_own)
        .transpose(0, 2, 1, 3)
        .reshape(dp_count, share_rows, hidden_own)
    )
    up_own, down_own = (
        lax.all_to_all(up_parts, "dp", split_axis=0, concat_axis=1, tiled=True),
        lax.all_to_all(down_parts, "dp", split_axis=0, concat_axis=1, tiled=True),
    )
    up_own = up_own.reshape(dp_count * share_rows, hidden_own)
    down_own = down_own.reshape(dp_count * share_rows, hidden_own)
    chosen = jnp.sum(
        (routes[:, :, None] == jnp.arange(E, dtype=jnp.int32)[None, None, :]).astype(jnp.float32),
        axis=1,
    )
    rows = jnp.arange(routes.shape[0], dtype=jnp.int32)
    earlier = (rows[None, :] < rows[:, None]).astype(jnp.bfloat16)
    before = jnp.dot(
        earlier, chosen.astype(jnp.bfloat16), preferred_element_type=jnp.float32
    ).astype(jnp.int32)
    slot_pos = jnp.sum(
        jnp.where(
            routes[:, :, None] == jnp.arange(E, dtype=jnp.int32)[None, None, :],
            before[:, None, :],
            0,
        ),
        axis=2,
    )
    target = routes * CAP + slot_pos
    slot_hits = jnp.arange(slots_all, dtype=jnp.int32)[:, None, None] == target[None, :, :]
    pick_table = jnp.sum(slot_hits.astype(jnp.float32), axis=2)
    weighted = jnp.sum(jnp.where(slot_hits, route_weights[None, :, :], 0.0), axis=2)
    x_local = jnp.dot(
        pick_table.astype(jnp.bfloat16), tokens, preferred_element_type=jnp.float32
    ).astype(jnp.bfloat16)
    d_local = jnp.dot(
        weighted, cotangent.astype(jnp.float32), precision=lax.Precision.HIGHEST
    ).astype(jnp.bfloat16)

    def spread(local):
        return jnp.broadcast_to(
            local.reshape(E, 1, CAP, features), (E, quarters, CAP, features)
        ).reshape(dp_count, CAP, features)

    def collect(returned):
        return jnp.sum(returned.reshape(E, quarters, CAP, features), axis=1).reshape(
            slots_all, features
        )

    x_in = lax.all_to_all(spread(x_local), "dp", split_axis=0, concat_axis=0, tiled=True).reshape(
        dp_count * CAP, features
    )
    partial_value = jnp.dot(x_in, up_own, preferred_element_type=jnp.float32).astype(jnp.bfloat16)
    pre_full = lax.psum(partial_value, "member").astype(jnp.float32)
    act_full = jax.nn.silu(pre_full).astype(jnp.bfloat16)
    y_part = contract(act_full, down_own, 1, 1)
    y_part, pre_full, act_full = (y_part, pre_full, act_full)
    y_back = lax.all_to_all(
        y_part.reshape(dp_count, CAP, features).astype(jnp.bfloat16),
        "dp",
        split_axis=0,
        concat_axis=0,
        tiled=True,
    ).astype(jnp.float32)
    d_in = lax.all_to_all(spread(d_local), "dp", split_axis=0, concat_axis=0, tiled=True).reshape(
        dp_count * CAP, features
    )
    d_act = lax.psum_scatter(
        contract(down_own, d_in, 0, 1).astype(jnp.bfloat16),
        "member",
        scatter_dimension=0,
        tiled=True,
    ).astype(jnp.float32)
    own_start = lax.axis_index("member") * per_member
    pre_share = lax.dynamic_slice_in_dim(pre_full, own_start, per_member, 1).T
    sigma = jax.nn.sigmoid(pre_share)
    d_share = (d_act * sigma * (1.0 + pre_share * (1.0 - sigma))).astype(jnp.bfloat16)
    d_pre = lax.all_gather(d_share, "member", axis=0, tiled=True)
    g_down = contract(d_in, act_full, 0, 0)
    g_up = contract(x_in, d_pre, 0, 1)
    dx_part = contract(d_pre, up_own, 0, 1)
    dx_part, g_up, g_down = (dx_part, g_up, g_down)
    dx_back = lax.all_to_all(
        dx_part.reshape(dp_count, CAP, features).astype(jnp.bfloat16),
        "dp",
        split_axis=0,
        concat_axis=0,
        tiled=True,
    ).astype(jnp.float32)
    y_slots = collect(y_back)
    dx_slots = collect(dx_back)
    mixed = jnp.dot(weighted.T, y_slots, precision=lax.Precision.HIGHEST).astype(jnp.bfloat16)
    grad_tokens = jnp.dot(pick_table.T, dx_slots, precision=lax.Precision.HIGHEST).astype(
        jnp.bfloat16
    )
    grad_up = g_up.astype(jnp.bfloat16).reshape(1, features, hidden_own)
    grad_down = g_down.astype(jnp.bfloat16).reshape(1, features, hidden_own)
    return (mixed, grad_tokens, grad_up, grad_down)


def solution(mesh):
    placed = (
        P("dp", "member"),
        P("dp", None),
        P("dp", None),
        P(None, ("member", "dp"), None),
        P(None, ("member", "dp"), None),
        P("dp", "member"),
    )
    return jax.shard_map(
        body,
        mesh=mesh,
        in_specs=placed,
        out_specs=(
            P("dp", "member"),
            P("dp", "member"),
            P("dp", "member", None),
            P("dp", "member", None),
        ),
        check_vma=False,
    )
```

profile of v0, /device:TPU:1, one launch (start us, length us, event | category | flops | bytes accessed | tf_op | source)
XLA Modules:
  0.0 533.1 jit_solution(2647584153746447925)
XLA Ops:
  11.4 16.7 %all-to-all-start.4 = ((bf16[32,34,256]{2,1,0:T(8,128)(2,1)}), bf16[32,34,256]{2,1,0:T(8,128)(2,1)S(1)}, u32[]{:S(2)}, u32[]{:S(2)}) async-start(bf16[32,34,256]{2,1,0:T(8,128)(2,1)} %bitcast.7), calls=%async_computation.4 | async-start | bytes 1310720 | tf_op jit(solution)/shard_map/all_to_all | solution.py:95
  29.2 38.0 %all-to-all-done.4 = bf16[32,34,256]{2,1,0:T(8,128)(2,1)S(1)} async-done(((bf16[32,34,256]{2,1,0:T(8,128)(2,1)}), bf16[32,34,256]{2,1,0:T(8,128)(2,1)S(1)}, u32[]{:S(2)}, u32[]{:S(2)}) %all-to-all-start.4) | async-done | bytes 557088 | tf_op jit(solution)/shard_map/all_to_all | solution.py:95
  68.1 4.1 all-to-all-start
  74.6 36.7 %all-to-all-done = bf16[32,34,256]{2,1,0:T(8,128)(2,1)S(1)} async-done(((bf16[32,34,256]{2,1,0:T(8,128)(2,1)}), bf16[32,34,256]{2,1,0:T(8,128)(2,1)S(1)}, u32[]{:S(2)}, u32[]{:S(2)}) %all-to-all-start) | async-done | bytes 557088 | tf_op jit(solution)/shard_map/all_to_all | solution.py:80
  112.1 4.5 all-to-all-start.2
  118.9 47.9 %all-to-all-done.2 = bf16[32,8,1792]{2,1,0:T(8,128)(2,1)S(1)} async-done(((bf16[32,8,1792]{2,1,0:T(8,128)(2,1)}), bf16[32,8,1792]{2,1,0:T(8,128)(2,1)S(1)}, u32[]{:S(2)}, u32[]{:S(2)}) %all-to-all-start.2) | async-done | bytes 917536 | tf_op jit(solution)/shard_map/all_to_all | solution.py:38
  166.9 4.5 all-to-all-start.1
  173.7 4.4 convolution_convert_fusion
  178.1 6.4 %copy.27 = bf16[1792,1088]{0,1:T(8,128)(2,1)} copy(bf16[1792,1088]{1,0:T(8,128)(2,1)} %convolution_convert_fusion) | data formatting | bytes 7798784 | tf_op jit(solution)/shard_map/convert_element_type | solution.py:99
  184.5 37.2 %all-to-all-done.1 = bf16[32,8,1792]{2,1,0:T(8,128)(2,1)S(1)} async-done(((bf16[32,8,1792]{2,1,0:T(8,128)(2,1)}), bf16[32,8,1792]{2,1,0:T(8,128)(2,1)S(1)}, u32[]{:S(2)}, u32[]{:S(2)}) %all-to-all-start.1) | async-done | bytes 917536 | tf_op jit(solution)/shard_map/all_to_all | solution.py:37
  221.7 3.1 convolution_convert_fusion.1
  226.8 156.5 %all-reduce.4.cloned.1.call-done = (bf16[1088,1792]{1,0:T(8,128)(2,1)}, bf16[1792,1088]{0,1:T(8,128)(2,1)}) async-done(((bf16[1088,1792]{1,0:T(8,128)(2,1)}, bf16[1792,1088]{0,1:T(8,128)(2,1)}), (bf16[1088,1792]{1,0:T(8,128)(2,1)}, bf16[1792,1088]{0,1:T(8,128)(2,1)})) %all-reduce.4.cloned.1.call-update) | async-done | bytes 7798800 | tf_op jit(solution)/shard_map/psum | solution.py:84
  388.3 5.0 multiply_convert_fusion
  393.3 6.9 %dot_general.42 = bf16[32,34,1792]{2,1,0:T(8,128)(2,1)} reshape(bf16[1088,1792]{1,0:T(8,128)(2,1)} %multiply_convert_fusion) | data formatting | bytes 7798784 | tf_op jit(solution)/shard_map/dot_general | solution.py:12
  400.3 4.6 convolution_convert_fusion.5
  404.8 13.0 %all-to-all-start.3 = ((bf16[32,34,256]{2,1,0:T(8,128)(2,1)}), bf16[32,34,256]{2,1,0:T(8,128)(2,1)S(1)}, u32[]{:S(2)}, u32[]{:S(2)}) async-start(bf16[32,34,256]{2,1,0:T(8,128)(2,1)} %convolution_convert_fusion.5), calls=%async_computation.3 | async-start | bytes 1310720 | tf_op jit(solution)/shard_map/all_to_all | solution.py:88
  417.9 37.0 %all-gather.2.cloned.1.call-done = bf16[1792,1088]{1,0:T(8,128)(2,1)} async-done(((bf16[112,1088]{1,0:T(8,128)(2,1)}), bf16[1792,1088]{1,0:T(8,128)(2,1)}) %all-gather.2.cloned.1.call-update) | async-done | bytes 3899408 | tf_op jit(solution)/shard_map/all_gather | solution.py:108
  454.9 6.4 %copy.29 = bf16[1088,1792]{1,0:T(8,128)(2,1)} copy(bf16[1088,1792]{0,1:T(8,128)(2,1)} %bitcast.65) | data formatting | bytes 7798784 | tf_op jit(solution)/shard_map/dot_general | solution.py:12
  461.3 6.9 %dot_general.48 = bf16[32,34,1792]{2,1,0:T(8,128)(2,1)} reshape(bf16[1088,1792]{1,0:T(8,128)(2,1)} %copy.29) | data formatting | bytes 7798784 | tf_op jit(solution)/shard_map/dot_general | solution.py:12
  468.2 4.7 convolution_convert_fusion.4
  472.9 13.0 %all-to-all-start.5 = ((bf16[32,34,256]{2,1,0:T(8,128)(2,1)}), bf16[32,34,256]{2,1,0:T(8,128)(2,1)S(1)}, u32[]{:S(2)}, u32[]{:S(2)}) async-start(bf16[32,34,256]{2,1,0:T(8,128)(2,1)} %convolution_convert_fusion.4), calls=%async_computation.5 | async-start | bytes 1310720 | tf_op jit(solution)/shard_map/all_to_all | solution.py:113
  485.9 4.4 fusion.1
  491.6 4.5 fusion
  496.2 28.9 %all-to-all-done.5 = bf16[32,34,256]{2,1,0:T(8,128)(2,1)S(1)} async-done(((bf16[32,34,256]{2,1,0:T(8,128)(2,1)}), bf16[32,34,256]{2,1,0:T(8,128)(2,1)S(1)}, u32[]{:S(2)}, u32[]{:S(2)}) %all-to-all-start.5) | async-done | bytes 557088 | tf_op jit(solution)/shard_map/all_to_all | solution.py:113
  (40 shorter events, 22.8 us)
Async XLA Ops:
  7.2 3.0 copy-start
  11.4 55.9 %all-to-all-start.4 = ((bf16[32,34,256]{2,1,0:T(8,128)(2,1)}), bf16[32,34,256]{2,1,0:T(8,128)(2,1)S(1)}, u32[]{:S(2)}, u32[]{:S(2)}) async-start(bf16[32,34,256]{2,1,0:T(8,128)(2,1)} %bitcast.7), calls=%async_computation.4 | async-start | bytes 1310720 | tf_op jit(solution)/shard_map/all_to_all | solution.py:95
  68.1 43.1 %all-to-all-start = ((bf16[32,34,256]{2,1,0:T(8,128)(2,1)}), bf16[32,34,256]{2,1,0:T(8,128)(2,1)S(1)}, u32[]{:S(2)}, u32[]{:S(2)}) async-start(bf16[32,34,256]{2,1,0:T(8,128)(2,1)} %bitcast), calls=%async_computation | async-start | bytes 1310720 | tf_op jit(solution)/shard_map/all_to_all | solution.py:80
  111.3 0.8 copy-start.2
  112.1 54.7 %all-to-all-start.2 = ((bf16[32,8,1792]{2,1,0:T(8,128)(2,1)}), bf16[32,8,1792]{2,1,0:T(8,128)(2,1)S(1)}, u32[]{:S(2)}, u32[]{:S(2)}) async-start(bf16[32,8,1792]{2,1,0:T(8,128)(2,1)} %bitcast.3), calls=%async_computation.2 | async-start | bytes 1835008 | tf_op jit(solution)/shard_map/all_to_all | solution.py:38
  166.9 54.8 %all-to-all-start.1 = ((bf16[32,8,1792]{2,1,0:T(8,128)(2,1)}), bf16[32,8,1792]{2,1,0:T(8,128)(2,1)S(1)}, u32[]{:S(2)}, u32[]{:S(2)}) async-start(bf16[32,8,1792]{2,1,0:T(8,128)(2,1)} %bitcast.1), calls=%async_computation.1 | async-start | bytes 1835008 | tf_op jit(solution)/shard_map/all_to_all | solution.py:37
  171.4 211.8 %all-reduce.4.cloned.1.call-start = ((), (), s32[]{:S(2)}) async-start(), calls=%async_computation.7 | async-start | bytes 15597568 | tf_op jit(solution)/shard_map/psum | solution.py:84
  224.8 230.1 %all-gather.2.cloned.1.call-start = ((), (), s32[]{:S(2)}) async-start(), calls=%async_computation.6 | async-start | bytes 4386816 | tf_op jit(solution)/shard_map/all_gather | solution.py:108
  404.8 68.1 %all-to-all-start.3 = ((bf16[32,34,256]{2,1,0:T(8,128)(2,1)}), bf16[32,34,256]{2,1,0:T(8,128)(2,1)S(1)}, u32[]{:S(2)}, u32[]{:S(2)}) async-start(bf16[32,34,256]{2,1,0:T(8,128)(2,1)} %convolution_convert_fusion.5), calls=%async_computation.3 | async-start | bytes 1310720 | tf_op jit(solution)/shard_map/all_to_all | solution.py:88
  468.2 17.7 %copy-start.3 = (bf16[1088,256]{1,0:T(8,128)(2,1)S(1)}, bf16[1088,256]{1,0:T(8,128)(2,1)}, u32[]{:S(2)}) copy-start(bf16[1088,256]{1,0:T(8,128)(2,1)} %reshape.88) | copy-start | bytes 1671172
  472.9 52.1 %all-to-all-start.5 = ((bf16[32,34,256]{2,1,0:T(8,128)(2,1)}), bf16[32,34,256]{2,1,0:T(8,128)(2,1)S(1)}, u32[]{:S(2)}, u32[]{:S(2)}) async-start(bf16[32,34,256]{2,1,0:T(8,128)(2,1)} %convolution_convert_fusion.4), calls=%async_computation.5 | async-start | bytes 1310720 | tf_op jit(solution)/shard_map/all_to_all | solution.py:113
  490.5 35.8 %copy-start.1 = (bf16[128,256]{1,0:T(8,128)(2,1)S(1)}, bf16[128,256]{1,0:T(8,128)(2,1)}, u32[]{:S(2)}) copy-start(bf16[128,256]{1,0:T(8,128)(2,1)} %param.11) | copy-start | bytes 196612
Sparse Core Ops, SparseCore 0:
  224.9 158.2 all-reduce.3
  388.4 66.4 all-gather.1
where the time goes:
time: 535 us; the launch traced here: 533 us
  waiting for transfers between devices  382 us (71%)
  starting transfers between devices  55.9 us (10%)
  local copies, waits for them, and re-layouts  36.6 us (7%)
  matrix products  29.3 us (5%)
  between operations  14.9 us (3%)
  other arithmetic  14.2 us (3%)
    psum x1, waiting for transfers between devices, body(): pre_full = lax.psum(partial_value, 'member').astype(jnp.float32)  156 us
    all_to_all x1, waiting for transfers between devices, body(): lax.all_to_all(down_parts, 'dp', split_axis=0, concat_axis=1, tiled=True)  47.9 us
    all_to_all x1, waiting for transfers between devices, body(): lax.all_to_all(spread(d_local), 'dp', split_axis=0, concat_axis=0, tiled=...  38 us
    all_to_all x1, waiting for transfers between devices, body(): lax.all_to_all(up_parts, 'dp', split_axis=0, concat_axis=1, tiled=True)  37.2 us
    all_gather x1, waiting for transfers between devices, body(): d_pre = lax.all_gather(d_share, 'member', axis=0, tiled=True)  37 us
    all_to_all x1, waiting for transfers between devices, body(): lax.all_to_all(spread(x_local), 'dp', split_axis=0, concat_axis=0, tiled=...  36.7 us
    all_to_all x1, waiting for transfers between devices, body(): lax.all_to_all(dx_part.reshape(dp_count, CAP, features).astype(jnp.bfloat...  28.9 us
    dot_general x5, matrix products, contract(): lax.dot_general(left, right, (((left_dim,), (right_dim,)), ((), ())), pre...  22.5 us
  transfers between devices with their start and end apart: 8, of which 7 were waited for; matrix products, arithmetic and copies ran while one was open for 12% of the time, Pallas kernels for 0%

commit v1 on v0

--- a/solution.py
+++ b/solution.py
@@ -6,6 +6,12 @@
 FF_W = 7168
 E = 8
 CAP = 34
+
+
+def gather_by_exchange(x, axis, dim):
+    size = lax.axis_size(axis)
+    repeats = [size if d == dim else 1 for d in range(x.ndim)]
+    return lax.all_to_all(jnp.tile(x, repeats), axis, split_axis=dim, concat_axis=dim, tiled=True)
 
 
 def contract(left, right, left_dim, right_dim):
@@ -105,7 +111,7 @@
     pre_share = lax.dynamic_slice_in_dim(pre_full, own_start, per_member, 1).T
     sigma = jax.nn.sigmoid(pre_share)
     d_share = (d_act * sigma * (1.0 + pre_share * (1.0 - sigma))).astype(jnp.bfloat16)
-    d_pre = lax.all_gather(d_share, "member", axis=0, tiled=True)
+    d_pre = gather_by_exchange(d_share, "member", 0)
     g_down = contract(d_in, act_full, 0, 0)
     g_up = contract(x_in, d_pre, 0, 1)
     dx_part = contract(d_pre, up_own, 0, 1)

time: 535 us -> 563 us (1.052)
  waiting for transfers between devices: 382 us -> 411 us
    all_to_all x0 -> x1, waiting for transfers between devices: none -> 44.9 us  [gather_by_exchange(): lax.all_to_all(jnp.tile(x, repeats), axis, split_axis=dim, concat_axis=di...]
    all_gather x1 -> x0, waiting for transfers between devices: 37 us -> none  [body(): d_pre = lax.all_gather(d_share, 'member', axis=0, tiled=True)]
    all_to_all x1, waiting for transfers between devices: 0.01 us -> 21 us  [body(): lax.all_to_all(y_part.reshape(dp_count, CAP, features).astype(jnp.bfloat1...]
    all_to_all x1, starting transfers between devices: 13 us -> 4.06 us  [body(): lax.all_to_all(dx_part.reshape(dp_count, CAP, features).astype(jnp.bfloat...]
  transfers between devices with their start and end apart: 8 -> 8, of which waited for: 7 -> 8; matrix products, arithmetic and copies ran while one was open for 12% -> 12% of each run, Pallas kernels for 0% -> 0%
where the time goes in v1:
time: 563 us; the launch traced here: 561 us
  waiting for transfers between devices  411 us (73%)
  starting transfers between devices  53.2 us (9%)
  local copies, waits for them, and re-layouts  38.1 us (7%)
  matrix products  29.4 us (5%)
  between operations  14.9 us (3%)
  other arithmetic  14.2 us (3%)
    psum x1, waiting for transfers between devices, body(): pre_full = lax.psum(partial_value, 'member').astype(jnp.float32)  156 us
    all_to_all x1, waiting for transfers between devices, body(): lax.all_to_all(down_parts, 'dp', split_axis=0, concat_axis=1, tiled=True)  47.9 us
    all_to_all x1, waiting for transfers between devices, gather_by_exchange(): lax.all_to_all(jnp.tile(x, repeats), axis, split_axis=dim, concat_axis=di...  44.9 us
    all_to_all x1, waiting for transfers between devices, body(): lax.all_to_all(spread(d_local), 'dp', split_axis=0, concat_axis=0, tiled=...  38 us
    all_to_all x1, waiting for transfers between devices, body(): lax.all_to_all(up_parts, 'dp', split_axis=0, concat_axis=1, tiled=True)  37.2 us
    all_to_all x1, waiting for transfers between devices, body(): lax.all_to_all(spread(x_local), 'dp', split_axis=0, concat_axis=0, tiled=...  36.7 us
    all_to_all x1, waiting for transfers between devices, body(): lax.all_to_all(dx_part.reshape(dp_count, CAP, features).astype(jnp.bfloat...  28.8 us
    dot_general x5, matrix products, contract(): lax.dot_general(left, right, (((left_dim,), (right_dim,)), ((), ())), pre...  22.6 us
  transfers between devices with their start and end apart: 8, of which 8 were waited for; matrix products, arithmetic and copies ran while one was open for 12% of the time, Pallas kernels for 0%

profile of v1, /device:TPU:1, one launch (start us, length us, event | category | flops | bytes accessed | tf_op | source)
XLA Modules:
  0.0 560.9 jit_solution(8641395452522870192)
XLA Ops:
  11.4 16.7 %all-to-all-start.4 = ((bf16[32,34,256]{2,1,0:T(8,128)(2,1)}), bf16[32,34,256]{2,1,0:T(8,128)(2,1)S(1)}, u32[]{:S(2)}, u32[]{:S(2)}) async-start(bf16[32,34,256]{2,1,0:T(8,128)(2,1)} %bitcast.7), calls=%async_computation.4 | async-start | bytes 1310720 | tf_op jit(solution)/shard_map/all_to_all | solution.py:101
  29.2 38.0 %all-to-all-done.4 = bf16[32,34,256]{2,1,0:T(8,128)(2,1)S(1)} async-done(((bf16[32,34,256]{2,1,0:T(8,128)(2,1)}), bf16[32,34,256]{2,1,0:T(8,128)(2,1)S(1)}, u32[]{:S(2)}, u32[]{:S(2)}) %all-to-all-start.4) | async-done | bytes 557088 | tf_op jit(solution)/shard_map/all_to_all | solution.py:101
  68.1 4.1 all-to-all-start
  74.6 36.7 %all-to-all-done = bf16[32,34,256]{2,1,0:T(8,128)(2,1)S(1)} async-done(((bf16[32,34,256]{2,1,0:T(8,128)(2,1)}), bf16[32,34,256]{2,1,0:T(8,128)(2,1)S(1)}, u32[]{:S(2)}, u32[]{:S(2)}) %all-to-all-start) | async-done | bytes 557088 | tf_op jit(solution)/shard_map/all_to_all | solution.py:86
  112.1 4.5 all-to-all-start.2
  118.9 47.9 %all-to-all-done.2 = bf16[32,8,1792]{2,1,0:T(8,128)(2,1)S(1)} async-done(((bf16[32,8,1792]{2,1,0:T(8,128)(2,1)}), bf16[32,8,1792]{2,1,0:T(8,128)(2,1)S(1)}, u32[]{:S(2)}, u32[]{:S(2)}) %all-to-all-start.2) | async-done | bytes 917536 | tf_op jit(solution)/shard_map/all_to_all | solution.py:44
  166.9 4.5 all-to-all-start.1
  173.7 4.4 convolution_convert_fusion
  178.1 6.4 %copy.29 = bf16[1792,1088]{0,1:T(8,128)(2,1)} copy(bf16[1792,1088]{1,0:T(8,128)(2,1)} %convolution_convert_fusion) | data formatting | bytes 7798784 | tf_op jit(solution)/shard_map/convert_element_type | solution.py:105
  184.5 37.2 %all-to-all-done.1 = bf16[32,8,1792]{2,1,0:T(8,128)(2,1)S(1)} async-done(((bf16[32,8,1792]{2,1,0:T(8,128)(2,1)}), bf16[32,8,1792]{2,1,0:T(8,128)(2,1)S(1)}, u32[]{:S(2)}, u32[]{:S(2)}) %all-to-all-start.1) | async-done | bytes 917536 | tf_op jit(solution)/shard_map/all_to_all | solution.py:43
  226.7 156.5 %all-reduce.4.cloned.1.call-done = (bf16[1088,1792]{1,0:T(8,128)(2,1)}, bf16[1792,1088]{0,1:T(8,128)(2,1)}) async-done(((bf16[1088,1792]{1,0:T(8,128)(2,1)}, bf16[1792,1088]{0,1:T(8,128)(2,1)}), (bf16[1088,1792]{1,0:T(8,128)(2,1)}, bf16[1792,1088]{0,1:T(8,128)(2,1)})) %all-reduce.4.cloned.1.call-update) | async-done | bytes 7798800 | tf_op jit(solution)/shard_map/psum | solution.py:90
  389.8 5.1 all-to-all-start.5
  394.9 5.0 multiply_convert_fusion
  400.0 6.9 %dot_general.42 = bf16[32,34,1792]{2,1,0:T(8,128)(2,1)} reshape(bf16[1088,1792]{1,0:T(8,128)(2,1)} %multiply_convert_fusion) | data formatting | bytes 7798784 | tf_op jit(solution)/shard_map/dot_general | solution.py:18
  406.9 4.6 convolution_convert_fusion.5
  411.5 44.9 %all-to-all-done.5 = bf16[16,112,1088]{2,1,0:T(8,128)(2,1)} async-done(((bf16[16,112,1088]{2,1,0:T(8,128)(2,1)}), bf16[16,112,1088]{2,1,0:T(8,128)(2,1)}, u32[]{:S(2)}, u32[]{:S(2)}) %all-to-all-start.5) | async-done | bytes 3899424 | tf_op jit(solution)/shard_map/all_to_all | solution.py:14
  456.4 14.2 %all-to-all-start.3 = ((bf16[32,34,256]{2,1,0:T(8,128)(2,1)}), bf16[32,34,256]{2,1,0:T(8,128)(2,1)S(1)}, u32[]{:S(2)}, u32[]{:S(2)}) async-start(bf16[32,34,256]{2,1,0:T(8,128)(2,1)} %convolution_convert_fusion.5), calls=%async_computation.3 | async-start | bytes 1310720 | tf_op jit(solution)/shard_map/all_to_all | solution.py:94
  470.5 6.4 %copy.31 = bf16[1088,1792]{1,0:T(8,128)(2,1)} copy(bf16[1088,1792]{0,1:T(8,128)(2,1)} %bitcast.10) | data formatting | bytes 7798784 | tf_op jit(solution)/shard_map/dot_general | solution.py:18
  476.9 6.9 %dot_general.48 = bf16[32,34,1792]{2,1,0:T(8,128)(2,1)} reshape(bf16[1088,1792]{1,0:T(8,128)(2,1)} %copy.31) | data formatting | bytes 7798784 | tf_op jit(solution)/shard_map/dot_general | solution.py:18
  483.9 4.7 convolution_convert_fusion.4
  488.6 21.0 %all-to-all-done.3 = bf16[32,34,256]{2,1,0:T(8,128)(2,1)S(1)} async-done(((bf16[32,34,256]{2,1,0:T(8,128)(2,1)}), bf16[32,34,256]{2,1,0:T(8,128)(2,1)S(1)}, u32[]{:S(2)}, u32[]{:S(2)}) %all-to-all-start.3) | async-done | bytes 557088 | tf_op jit(solution)/shard_map/all_to_all | solution.py:94
  513.7 4.4 fusion.1
  519.4 4.5 fusion
  523.9 28.8 %all-to-all-done.6 = bf16[32,34,256]{2,1,0:T(8,128)(2,1)S(1)} async-done(((bf16[32,34,256]{2,1,0:T(8,128)(2,1)}), bf16[32,34,256]{2,1,0:T(8,128)(2,1)S(1)}, u32[]{:S(2)}, u32[]{:S(2)}) %all-to-all-start.6) | async-done | bytes 557088 | tf_op jit(solution)/shard_map/all_to_all | solution.py:119
  (40 shorter events, 31.5 us)
Async XLA Ops:
  7.2 3.0 copy-start
  11.4 55.9 %all-to-all-start.4 = ((bf16[32,34,256]{2,1,0:T(8,128)(2,1)}), bf16[32,34,256]{2,1,0:T(8,128)(2,1)S(1)}, u32[]{:S(2)}, u32[]{:S(2)}) async-start(bf16[32,34,256]{2,1,0:T(8,128)(2,1)} %bitcast.7), calls=%async_computation.4 | async-start | bytes 1310720 | tf_op jit(solution)/shard_map/all_to_all | solution.py:101
  68.1 43.1 %all-to-all-start = ((bf16[32,34,256]{2,1,0:T(8,128)(2,1)}), bf16[32,34,256]{2,1,0:T(8,128)(2,1)S(1)}, u32[]{:S(2)}, u32[]{:S(2)}) async-start(bf16[32,34,256]{2,1,0:T(8,128)(2,1)} %bitcast), calls=%async_computation | async-start | bytes 1310720 | tf_op jit(solution)/shard_map/all_to_all | solution.py:86
  111.3 0.8 copy-start.2
  112.1 54.7 %all-to-all-start.2 = ((bf16[32,8,1792]{2,1,0:T(8,128)(2,1)}), bf16[32,8,1792]{2,1,0:T(8,128)(2,1)S(1)}, u32[]{:S(2)}, u32[]{:S(2)}) async-start(bf16[32,8,1792]{2,1,0:T(8,128)(2,1)} %bitcast.3), calls=%async_computation.2 | async-start | bytes 1835008 | tf_op jit(solution)/shard_map/all_to_all | solution.py:44
  166.9 54.8 %all-to-all-start.1 = ((bf16[32,8,1792]{2,1,0:T(8,128)(2,1)}), bf16[32,8,1792]{2,1,0:T(8,128)(2,1)S(1)}, u32[]{:S(2)}, u32[]{:S(2)}) async-start(bf16[32,8,1792]{2,1,0:T(8,128)(2,1)} %bitcast.1), calls=%async_computation.1 | async-start | bytes 1835008 | tf_op jit(solution)/shard_map/all_to_all | solution.py:43
  171.4 211.8 %all-reduce.4.cloned.1.call-start = ((), (), s32[]{:S(2)}) async-start(), calls=%async_computation.7 | async-start | bytes 15597568 | tf_op jit(solution)/shard_map/psum | solution.py:90
  389.8 66.6 %all-to-all-start.5 = ((bf16[16,112,1088]{2,1,0:T(8,128)(2,1)}), bf16[16,112,1088]{2,1,0:T(8,128)(2,1)}, u32[]{:S(2)}, u32[]{:S(2)}) async-start(bf16[16,112,1088]{2,1,0:T(8,128)(2,1)} %tile.2), calls=%async_computation.5 | async-start | bytes 8257536 | tf_op jit(solution)/shard_map/all_to_all | solution.py:14
  456.4 53.3 %all-to-all-start.3 = ((bf16[32,34,256]{2,1,0:T(8,128)(2,1)}), bf16[32,34,256]{2,1,0:T(8,128)(2,1)S(1)}, u32[]{:S(2)}, u32[]{:S(2)}) async-start(bf16[32,34,256]{2,1,0:T(8,128)(2,1)} %convolution_convert_fusion.5), calls=%async_computation.3 | async-start | bytes 1310720 | tf_op jit(solution)/shard_map/all_to_all | solution.py:94
  483.9 29.8 %copy-start.3 = (bf16[1088,256]{1,0:T(8,128)(2,1)S(1)}, bf16[1088,256]{1,0:T(8,128)(2,1)}, u32[]{:S(2)}) copy-start(bf16[1088,256]{1,0:T(8,128)(2,1)} %reshape.95) | copy-start | bytes 1671172
  509.6 43.1 %all-to-all-start.6 = ((bf16[32,34,256]{2,1,0:T(8,128)(2,1)}), bf16[32,34,256]{2,1,0:T(8,128)(2,1)S(1)}, u32[]{:S(2)}, u32[]{:S(2)}) async-start(bf16[32,34,256]{2,1,0:T(8,128)(2,1)} %convolution_convert_fusion.4), calls=%async_computation.6 | async-start | bytes 1310720 | tf_op jit(solution)/shard_map/all_to_all | solution.py:119
  519.4 34.7 %copy-start.1 = (bf16[128,256]{1,0:T(8,128)(2,1)S(1)}, bf16[128,256]{1,0:T(8,128)(2,1)}, u32[]{:S(2)}) copy-start(bf16[128,256]{1,0:T(8,128)(2,1)} %param.11) | copy-start | bytes 196612
Sparse Core Ops, SparseCore 0:
  224.9 158.2 all-reduce.3
